TPU v7x, 512 devices: a whole 4x8x8 slice. The times are simulated.
512 devices in a mesh: ka: 8 (over y_hi, core), pb: 16 (over y_lo, z), row: 4 (over x).
Axes of the slice: x: 4, y: 8 (y_hi: 4, y_lo: 2; y = y_hi * 2 + y_lo), z: 8, core: 2. Of those that a mesh axis runs over, the one named last changes fastest.
Arguments:
- coupling: bfloat16 [64, 64, 20736], P('pb', ('ka', 'row')), may hold values from -1 to 1
- rotation: bfloat16 [64, 36, 36], P('pb'), may hold values from -1 to 1
- freq: float32 [64, 36], P('pb'), may hold values from 0.02 to 0.3
- eigvec: bfloat16 [1024, 24, 24], P(('ka', 'row')), may hold values from -1.25 to 1.25
- energies: float32 [1024, 24], P(('ka', 'row')), may hold values from -1.5 to 1.5
- window: int32 [1024], P(('ka', 'row')), may hold values from 12 to 24
- kq_index: int32 [64, 1024], P('pb'), may hold values from 0 to 1023, as said below
- kpoints: float32 [1024, 3], replicated, may hold values from 0 to 1
- lattice: int32 [64, 3], replicated, may hold values from -3 to 3
Outputs:
- electron: float32 [1024, 24], P(('ka', 'row'))
- phonon: float32 [64, 36], P('pb')
Inputs may be any that keep to these rules, and one draw needn't show every extreme that they name: The k-points form a shifted grid of 1024 points, (1024 // 64) x 8 x 8, listed in an order drawn from the seed; each q-point is a vector of that grid without the shift. kq_index[q, k] is the index of the k-point equal to kpoints[k] plus the q-point's vector modulo 1, so each row of kq_index is a permutation of 0 to 1023.
All inputs are finite; a program needn't handle non-finite values.
Results may differ from a plain program's by a relative error of at most 0.00089.
Values may be sent and summed in bfloat16 or wider, within the bound.
A program may use at most 128 MiB of HBM per device.

v0:
```python
import math
import jax
import jax.numpy as jnp
from jax import lax
from jax.sharding import PartitionSpec as P

SIGMA = 0.1
THERMAL_ENERGY_KT = 0.2


def phase_table(lattice, kpoint_rows):
    rvec = lattice.astype(jnp.float32)
    argument = (
        rvec[:, 0:1] * kpoint_rows[:, 0][None, :]
        + rvec[:, 1:2] * kpoint_rows[:, 1][None, :]
        + rvec[:, 2:3] * kpoint_rows[:, 2][None, :]
    )
    return jnp.cos(2.0 * math.pi * argument).astype(jnp.bfloat16)


def block_terms(
    coup_rows, phase_cols, rot_rows, freq_rows, eig_k, eig_kq, level_k, level_kq, lim_k, lim_kq
):
    q_block = coup_rows.shape[0]
    k_block = phase_cols.shape[1]
    columns = q_block * k_block
    n_modes = rot_rows.shape[1]
    n_bands = eig_k.shape[0]
    norm = 1.0 / (math.sqrt(2.0 * math.pi) * SIGMA)
    bloch = jnp.einsum(
        "qrf,rk->fqk", coup_rows, phase_cols, preferred_element_type=jnp.float32
    ).astype(jnp.bfloat16)
    bloch = bloch.reshape(n_modes, n_bands, n_bands, columns)
    rot_cols = jnp.repeat(jnp.transpose(rot_rows, (1, 2, 0)), k_block, axis=2)
    modal = jnp.einsum(
        "amnc,abc->bmnc", bloch, rot_cols, preferred_element_type=jnp.float32
    ).astype(jnp.bfloat16)
    eig_k_cols = jnp.tile(eig_k, (1, 1, q_block))
    right = jnp.einsum(
        "bmjc,jnc->bmnc", modal, eig_k_cols, preferred_element_type=jnp.float32
    ).astype(jnp.bfloat16)
    coupled = jnp.einsum("imc,binc->bmnc", eig_kq, right, preferred_element_type=jnp.float32)
    level_k_cols = jnp.tile(level_k, (1, q_block))
    lim_k_cols = jnp.tile(lim_k, (q_block,))
    freq_cols = jnp.repeat(freq_rows.T, k_block, axis=1)
    diff = level_kq[None, :, None, :] - level_k_cols[None, None, :, :] - freq_cols[:, None, None, :]
    delta = jnp.exp(-(diff * diff) / (2.0 * SIGMA * SIGMA)) * norm
    bands = jnp.arange(n_bands).astype(jnp.float32)
    mask_m = (bands[:, None] < lim_kq[None, :]).astype(jnp.float32)
    mask_n = (bands[:, None] < lim_k_cols[None, :]).astype(jnp.float32)
    strength = coupled * coupled * delta * mask_m[None, :, None, :] * mask_n[None, None, :, :]
    filling_initial = jax.nn.sigmoid(-level_k_cols / THERMAL_ENERGY_KT)
    filling_final = jax.nn.sigmoid(-level_kq / THERMAL_ENERGY_KT)
    elec = jnp.sum(strength, axis=(0, 1)).reshape(n_bands, q_block, k_block).sum(axis=1)
    phon = jnp.sum(
        strength * (filling_initial[None, None, :, :] - filling_final[None, :, None, :]),
        axis=(1, 2),
    )
    phon = phon.reshape(n_modes, q_block, k_block).sum(axis=2)
    return (elec, phon)


def on_device(coupling, rotation, freq, eigvec, energies, window, kq_index, kpoints, lattice):
    n_ka = lax.axis_size("ka")
    n_row = lax.axis_size("row")
    n_pb = lax.axis_size("pb")
    k_dev = eigvec.shape[0]
    q_dev = rotation.shape[0]
    n_bands = eigvec.shape[1]
    n_modes = rotation.shape[1]
    total_k = k_dev * n_ka * n_row
    total_q = q_dev * n_pb
    eigen_grid = lax.all_gather(eigvec, ("ka", "row"), axis=0, tiled=True)
    level_all, limit_all = (
        lax.all_gather(energies, ("ka", "row"), axis=0, tiled=True),
        lax.all_gather(window.astype(jnp.float32), ("ka", "row"), axis=0, tiled=True),
    )
    eig_cols = jnp.transpose(eigen_grid, (1, 2, 0))
    level_cols = level_all.T
    ka_pos = lax.axis_index("ka")
    row_pos = lax.axis_index("row")
    coup_full = lax.all_gather(coupling, ("ka", "row"), axis=1, tiled=True)
    q_start = jnp.int32(0)
    k_start = (ka_pos * n_row + row_pos) * k_dev
    kq_mine = lax.dynamic_slice(kq_index, (q_start, k_start), (q_dev, k_dev))
    kp_mine = lax.dynamic_slice(kpoints, (k_start, jnp.int32(0)), (k_dev, 3))
    eig_mine = lax.dynamic_slice_in_dim(eig_cols, k_start, k_dev, 2)
    lev_mine = lax.dynamic_slice_in_dim(level_cols, k_start, k_dev, 1)
    lim_mine = lax.dynamic_slice_in_dim(limit_all, k_start, k_dev, 0)
    phase_all = phase_table(lattice, kp_mine)
    k_block = min(k_dev, 128)
    elec_cols = [None] * (k_dev // k_block)
    index = kq_mine.reshape(-1)
    eig_kq = jnp.take(eig_cols, index, axis=2)
    level_kq = jnp.take(level_cols, index, axis=1)
    lim_kq = jnp.take(limit_all, index, axis=0)
    elec, phon = block_terms(
        coup_full, phase_all, rotation, freq, eig_mine, eig_kq, lev_mine, level_kq, lim_mine, lim_kq
    )
    elec_cols[0] = elec
    elec_local = elec_cols[0].T * (1.0 / (total_q * n_modes * n_bands))
    phon_local = phon.T * (1.0 / (total_k * n_bands))
    phonon = lax.psum(phon_local, ("ka", "row"))
    electron = lax.psum(elec_local, "pb")
    return (electron, phonon)


def solution(mesh):
    return jax.shard_map(
        on_device,
        mesh=mesh,
        in_specs=(
            P("pb", ("ka", "row"), None),
            P("pb", None, None),
            P("pb", None),
            P(("ka", "row"), None, None),
            P(("ka", "row"), None),
            P(("ka", "row")),
            P("pb", None),
            P(),
            P(),
        ),
        out_specs=(P(("ka", "row"), None), P("pb", None)),
        check_vma=False,
    )
```

profile of v0, /device:TPU:40, one launch (start us, length us, event | category | flops | bytes accessed | tf_op | source)
XLA Modules:
  0.0 554.0 jit_solution(66930285304489676)
XLA Ops:
  7.2 1.7 copy.47
  9.0 1.8 copy.49
  11.2 0.7 convert_element_type.50
  11.8 1.3 dynamic-slice.8
  13.8 0.8 convert_dynamic-update-slice_fusion
  14.5 78.9 %all-reduce = f32[1024]{0:T(1024)S(1)} all-reduce(f32[1024]{0:T(1024)S(1)} %convert_dynamic-update-slice_fusion), channel_id=1, replica_groups=mesh['ka'=8,'pb'=16,'row'=4] {'ka','row'}, use_global_device_ids=true, to_apply=%add | all-reduce | flops 1024 | bytes 8192
  93.6 1.0 gather_fusion.2
  94.6 0.8 copy.79
  95.5 0.1 copy.62
  95.7 82.7 %all-gather = f32[32,32,24]{1,2,0:T(8,128)S(1)} all-gather(f32[1,32,24]{1,2,0:T(8,128)} %bitcast.93), channel_id=1, replica_groups=mesh['ka'=8,'pb'=16,'row'=4] {'ka','row'}, dimensions={0}, use_global_device_ids=true | all-gather | bytes 101376 | tf_op jit(solution)/shard_map/all_gather | solution.py:75
  178.4 0.2 copy.57
  178.8 0.1 copy.61
  178.9 0.1 copy.64
  179.0 0.7 gather_fusion.1
  179.8 0.1 copy.65
  179.9 0.1 copy.59
  180.0 0.8 constant_dynamic-slice_fusion.1
  180.8 2.2 broadcast_subtract_fusion
  182.9 0.9 dynamic-slice_bitcast_fusion
  183.9 0.1 copy.48
  184.0 3.5 gather_fusion
  187.6 8.0 %fusion.4 = bf16[20736,4,32]{0,2,1:T(8,128)(2,1)} fusion(bf16[4,64,20736]{2,0,1:T(4,128)(2,1)} %all-gather.6.cloned.1.call-done, f32[32]{0:T(128)S(1)} %get-tuple-element.18, f32[64]{0:T(128)S(1)} %get-tuple-element.15, f32[32]{0:T(128)S(1)} %get-tuple-element.19, f32[64]{0:T(128)S(1)} %get-tuple-element.16, f32[32]{0:T(128)S(1)} %get-tuple-element.17, ...), kind=kOutput, calls=%fused_computation.10 | convolution fusion | flops 342407168 | bytes 15926400 | tf_op jit(solution)/shard_map/qrf,rk->fqk/dot_general | solution.py:30
  195.6 47.2 %reshape.253 = bf16[36,24,24,128]{2,1,0,3:T(8,128)(2,1)} reshape(bf16[20736,4,32]{0,2,1:T(8,128)(2,1)} %fusion.4) | data formatting | bytes 10616832 | tf_op jit(solution)/shard_map/reshape | solution.py:33
  242.8 0.1 tile.10
  242.9 0.2 broadcast_in_dim.40.clone
  243.1 23.0 %convert_bitcast_fusion = bf16[36,24,24,128]{0,2,1,3:T(8,128)(2,1)} fusion(bf16[24,24,128,1]{0,1,3,2:T(8,128)(2,1)S(1)} %bitcast.86, bf16[36,36,128,1]{1,0,3,2:T(8,128)(2,1)S(1)} %bitcast.85, bf16[36,24,24,128]{2,1,0,3:T(8,128)(2,1)} %reshape.253), kind=kOutput, calls=%fused_computation.15 | convolution fusion | flops 323813376 | bytes 11096064 | tf_op jit(solution)/shard_map/bmjc,jnc->bmnc/dot_general | solution.py:39
  266.1 69.3 %multiply_reduce_fusion = (f32[36,128]{0,1:T(8,128)S(1)}, f32[24,128]{0,1:T(8,128)S(1)}) fusion(f32[24,24,128]{0,1,2:T(8,128)} %get-tuple-element.22, f32[24,128]{0,1:T(8,128)S(1)} %copy.63, f32[24,128]{0,1:T(8,128)S(1)} %copy.62, f32[36,128]{0,1:T(8,128)S(1)} %bitcast.90, f32[24,24,128]{0,1,2:T(8,128)} %get-tuple-element.23, ...), kind=kOutput, calls=%fused_computation.6 | convolution fusion | flops 159318528 | bytes 6119552 | tf_op jit(solution)/shard_map/imc,binc->bmnc/dot_general | solution.py:42
  335.5 69.8 %psum.14 = f32[32,24]{1,0:T(8,128)S(1)} all-reduce(f32[32,24]{1,0:T(8,128)S(1)} %multiply_bitcast_fusion.1), channel_id=1, replica_groups=mesh['ka'=8,'pb'=16,'row'=4] {'pb'}, use_global_device_ids=true, to_apply=%region_2.3 | all-reduce | flops 768 | bytes 6144 | tf_op jit(solution)/shard_map/psum | solution.py:104
  405.3 0.7 copy.67
  405.9 0.1 copy.78
  406.0 140.5 %psum.15 = f32[4,36]{0,1:T(8,128)S(1)} all-reduce(f32[4,36]{0,1:T(8,128)S(1)} %multiply_bitcast_fusion), channel_id=1, replica_groups=mesh['ka'=8,'pb'=16,'row'=4] {'ka','row'}, use_global_device_ids=true, to_apply=%region_5.6 | all-reduce | flops 144 | bytes 1152 | tf_op jit(solution)/shard_map/psum | solution.py:103
  546.5 0.7 copy.68
  (39 shorter events, 1.1 us)
Async XLA Ops:
  7.2 3.7 copy-start
  7.2 175.7 %all-gather.4.cloned.1.call-start = ((), (), s32[]{:S(2)}) async-start(), calls=%async_computation | async-start | bytes 6488064 | tf_op jit(solution)/shard_map/all_gather | solution.py:73
  9.0 178.6 %all-gather.6.cloned.1.call-start = ((), (), s32[]{:S(2)}) async-start(), calls=%async_computation.1 | async-start | bytes 10948608 | tf_op jit(solution)/shard_map/all_gather | solution.py:82
  243.1 23.0 %copy-start.2 = (f32[4,36]{1,0:T(4,128)S(1)}, f32[4,36]{1,0:T(4,128)}, u32[]{:S(2)}) copy-start(f32[4,36]{1,0:T(4,128)} %param.11) | copy-start | bytes 1732
  266.1 281.1 %copy-start.1 = (s32[4,1024]{1,0:T(4,128)S(1)}, s32[4,1024]{1,0:T(4,128)}, u32[]{:S(2)}) copy-start(s32[4,1024]{1,0:T(4,128)} %param.15) | copy-start | bytes 49156
Sparse Core Ops, SparseCore 0:
  11.1 75.5 all-gather.3
  89.9 93.6 all-gather.5
where the time goes:
time: 555 us; the launch traced here: 554 us
  blocking collectives  372 us (67%)
  matrix products  100 us (18%)
  local copies, waits for them, and re-layouts  63 us (11%)
  between operations  14.9 us (3%)
    psum x1, blocking collectives, on_device(): phonon = lax.psum(phon_local, ('ka', 'row'))  140 us
    all_gather x1, blocking collectives, on_device(): lax.all_gather(energies, ('ka', 'row'), axis=0, tiled=True)  82.7 us
    unnamed x1, blocking collectives  78.9 us
    psum x1, blocking collectives, on_device(): electron = lax.psum(elec_local, 'pb')  69.8 us
    dot_general x1, matrix products, block_terms(): jnp.einsum('imc,binc->bmnc', eig_kq, right, preferred_element_type=jnp.fl...  69.3 us
    reshape x1, local copies, waits for them, and re-layouts, block_terms(): bloch = bloch.reshape(n_modes, n_bands, n_bands, columns)  47.2 us
    dot_general x1, matrix products, block_terms(): jnp.einsum('bmjc,jnc->bmnc', modal, eig_k_cols, preferred_element_type=jn...  23 us
  transfers between devices with their start and end apart: 2, of which 0 were waited for; matrix products, arithmetic and copies ran while one was open for 3% of the time, Pallas kernels for 0%

commit v1 on v0

--- a/solution.py
+++ b/solution.py
@@ -101,7 +101,7 @@
     elec_local = elec_cols[0].T * (1.0 / (total_q * n_modes * n_bands))
     phon_local = phon.T * (1.0 / (total_k * n_bands))
     phonon = lax.psum(phon_local, ("ka", "row"))
-    electron = lax.psum(elec_local, "pb")
+    electron = jnp.sum(lax.all_gather(elec_local, "pb"), axis=0)
     return (electron, phonon)
 
 

time: 555 us -> 525 us (0.946)
  blocking collectives: 372 us -> 343 us
    psum x1 -> x0, blocking collectives: 69.8 us -> none  [on_device(): electron = lax.psum(elec_local, 'pb')]
    all_gather x0 -> x1, blocking collectives: none -> 42.2 us  [on_device(): electron = jnp.sum(lax.all_gather(elec_local, 'pb'), axis=0)]
where the time goes in v1:
time: 525 us
  blocking collectives  343 us (65%)
  matrix products  100 us (19%)
  local copies, waits for them, and re-layouts  62.4 us (12%)
  between operations  14.9 us (3%)
    psum x1, blocking collectives, on_device(): phonon = lax.psum(phon_local, ('ka', 'row'))  139 us
    all_gather x1, blocking collectives, on_device(): lax.all_gather(energies, ('ka', 'row'), axis=0, tiled=True)  82.7 us
    unnamed x1, blocking collectives  78.9 us
    dot_general x1, matrix products, block_terms(): jnp.einsum('imc,binc->bmnc', eig_kq, right, preferred_element_type=jnp.fl...  69.3 us
    reshape x1, local copies, waits for them, and re-layouts, block_terms(): bloch = bloch.reshape(n_modes, n_bands, n_bands, columns)  47.2 us
    all_gather x1, blocking collectives, on_device(): electron = jnp.sum(lax.all_gather(elec_local, 'pb'), axis=0)  42.2 us
    dot_general x1, matrix products, block_terms(): jnp.einsum('bmjc,jnc->bmnc', modal, eig_k_cols, preferred_element_type=jn...  23 us
  transfers between devices with their start and end apart: 2, of which 0 were waited for; matrix products, arithmetic and copies ran while one was open for 3% of the time, Pallas kernels for 0%

profile of v1, /device:TPU:40, one launch (start us, length us, event | category | flops | bytes accessed | tf_op | source)
XLA Modules:
  0.0 524.8 jit_solution(6063365332447195264)
XLA Ops:
  7.2 1.7 copy.47
  9.0 1.8 copy.49
  11.2 0.7 convert_element_type.50
  11.8 1.3 dynamic-slice.8
  13.8 0.8 convert_dynamic-update-slice_fusion
  14.5 78.9 %all-reduce = f32[1024]{0:T(1024)S(1)} all-reduce(f32[1024]{0:T(1024)S(1)} %convert_dynamic-update-slice_fusion), channel_id=1, replica_groups=mesh['ka'=8,'pb'=16,'row'=4] {'ka','row'}, use_global_device_ids=true, to_apply=%add | all-reduce | flops 1024 | bytes 8192
  93.6 1.0 gather_fusion.2
  94.6 0.8 copy.79
  95.5 0.1 copy.62
  95.7 82.7 %all-gather.1 = f32[32,32,24]{1,2,0:T(8,128)S(1)} all-gather(f32[1,32,24]{1,2,0:T(8,128)} %bitcast.95), channel_id=1, replica_groups=mesh['ka'=8,'pb'=16,'row'=4] {'ka','row'}, dimensions={0}, use_global_device_ids=true | all-gather | bytes 101376 | tf_op jit(solution)/shard_map/all_gather | solution.py:75
  178.4 0.2 copy.57
  178.8 0.1 copy.61
  178.9 0.1 copy.65
  179.0 0.7 gather_fusion.1
  179.8 0.1 copy.66
  179.9 0.1 copy.59
  180.0 0.8 constant_dynamic-slice_fusion.1
  180.8 2.2 broadcast_subtract_fusion
  182.9 0.9 dynamic-slice_bitcast_fusion
  183.9 0.1 copy.48
  184.0 3.5 gather_fusion
  187.6 8.0 %fusion.4 = bf16[20736,4,32]{0,2,1:T(8,128)(2,1)} fusion(bf16[4,64,20736]{2,0,1:T(4,128)(2,1)} %all-gather.8.cloned.1.call-done, f32[32]{0:T(128)S(1)} %get-tuple-element.18, f32[64]{0:T(128)S(1)} %get-tuple-element.15, f32[32]{0:T(128)S(1)} %get-tuple-element.19, f32[64]{0:T(128)S(1)} %get-tuple-element.16, f32[32]{0:T(128)S(1)} %get-tuple-element.17, ...), kind=kOutput, calls=%fused_computation.10 | convolution fusion | flops 342407168 | bytes 15926400 | tf_op jit(solution)/shard_map/qrf,rk->fqk/dot_general | solution.py:30
  195.6 47.2 %reshape.257 = bf16[36,24,24,128]{2,1,0,3:T(8,128)(2,1)} reshape(bf16[20736,4,32]{0,2,1:T(8,128)(2,1)} %fusion.4) | data formatting | bytes 10616832 | tf_op jit(solution)/shard_map/reshape | solution.py:33
  242.8 0.1 tile.10
  242.9 0.2 broadcast_in_dim.40.clone
  243.1 23.0 %convert_bitcast_fusion = bf16[36,24,24,128]{0,2,1,3:T(8,128)(2,1)} fusion(bf16[24,24,128,1]{0,1,3,2:T(8,128)(2,1)S(1)} %bitcast.88, bf16[36,36,128,1]{1,0,3,2:T(8,128)(2,1)S(1)} %bitcast.87, bf16[36,24,24,128]{2,1,0,3:T(8,128)(2,1)} %reshape.257), kind=kOutput, calls=%fused_computation.15 | convolution fusion | flops 323813376 | bytes 11096064 | tf_op jit(solution)/shard_map/bmjc,jnc->bmnc/dot_general | solution.py:39
  266.1 69.3 %multiply_reduce_fusion = (f32[36,128]{0,1:T(8,128)S(1)}, f32[24,128]{0,1:T(8,128)S(1)}) fusion(f32[24,24,128]{0,1,2:T(8,128)} %get-tuple-element.22, f32[24,128]{0,1:T(8,128)S(1)} %copy.63, f32[24,128]{0,1:T(8,128)S(1)} %copy.62, f32[36,128]{0,1:T(8,128)S(1)} %bitcast.92, f32[24,24,128]{0,1,2:T(8,128)} %get-tuple-element.23, ...), kind=kOutput, calls=%fused_computation.6 | convolution fusion | flops 159318528 | bytes 6119552 | tf_op jit(solution)/shard_map/imc,binc->bmnc/dot_general | solution.py:42
  335.5 0.1 copy.78
  335.6 138.9 %psum.7 = f32[4,36]{0,1:T(8,128)S(1)} all-reduce(f32[4,36]{0,1:T(8,128)S(1)} %multiply_bitcast_fusion), channel_id=1, replica_groups=mesh['ka'=8,'pb'=16,'row'=4] {'ka','row'}, use_global_device_ids=true, to_apply=%region_5.6 | all-reduce | flops 144 | bytes 1152 | tf_op jit(solution)/shard_map/psum | solution.py:103
  474.5 0.7 copy.68
  475.2 42.2 %all-gather.2 = f32[16,32,24]{1,2,0:T(8,128)S(1)} all-gather(f32[1,32,24]{1,2,0:T(8,128)S(1)} %copy.64), channel_id=2, replica_groups=mesh['ka'=8,'pb'=16,'row'=4] {'pb'}, dimensions={0}, use_global_device_ids=true | all-gather | bytes 52224 | tf_op jit(solution)/shard_map/all_gather | solution.py:104
  517.4 0.6 reduce_sum.47
  (40 shorter events, 1.2 us)
Async XLA Ops:
  7.2 3.7 copy-start
  7.2 175.7 %all-gather.6.cloned.1.call-start = ((), (), s32[]{:S(2)}) async-start(), calls=%async_computation | async-start | bytes 6488064 | tf_op jit(solution)/shard_map/all_gather | solution.py:73
  9.0 178.6 %all-gather.8.cloned.1.call-start = ((), (), s32[]{:S(2)}) async-start(), calls=%async_computation.1 | async-start | bytes 10948608 | tf_op jit(solution)/shard_map/all_gather | solution.py:82
  243.1 23.0 %copy-start.2 = (f32[4,36]{1,0:T(4,128)S(1)}, f32[4,36]{1,0:T(4,128)}, u32[]{:S(2)}) copy-start(f32[4,36]{1,0:T(4,128)} %param.11) | copy-start | bytes 1732
  266.1 251.9 %copy-start.1 = (s32[4,1024]{1,0:T(4,128)S(1)}, s32[4,1024]{1,0:T(4,128)}, u32[]{:S(2)}) copy-start(s32[4,1024]{1,0:T(4,128)} %param.15) | copy-start | bytes 49156
Sparse Core Ops, SparseCore 0:
  11.1 75.5 all-gather.5
  89.9 93.6 all-gather.7

commit v2 on v0

--- a/solution.py
+++ b/solution.py
@@ -100,7 +100,7 @@
     elec_cols[0] = elec
     elec_local = elec_cols[0].T * (1.0 / (total_q * n_modes * n_bands))
     phon_local = phon.T * (1.0 / (total_k * n_bands))
-    phonon = lax.psum(phon_local, ("ka", "row"))
+    phonon = lax.psum(lax.psum(phon_local, "row"), "ka")
     electron = lax.psum(elec_local, "pb")
     return (electron, phonon)
 

time: 555 us -> 458 us (0.83)
  blocking collectives: 372 us -> 275 us
    psum x1 -> x2, blocking collectives: 140 us -> 43.7 us  [on_device(): phonon = lax.psum(lax.psum(phon_local, 'row'), 'ka')]
  transfers between devices with their start and end apart: 2 -> 2, of which waited for: 0 -> 0; matrix products, arithmetic and copies ran while one was open for 3% -> 4% of each run, Pallas kernels for 0% -> 0%
where the time goes in v2:
time: 458 us; the launch traced here: 457 us
  blocking collectives  275 us (60%)
  matrix products  100 us (22%)
  local copies, waits for them, and re-layouts  63 us (14%)
  between operations  14.9 us (3%)
    all_gather x1, blocking collectives, on_device(): lax.all_gather(energies, ('ka', 'row'), axis=0, tiled=True)  82.7 us
    unnamed x1, blocking collectives  78.9 us
    psum x1, blocking collectives, on_device(): electron = lax.psum(elec_local, 'pb')  69.8 us
    dot_general x1, matrix products, block_terms(): jnp.einsum('imc,binc->bmnc', eig_kq, right, preferred_element_type=jnp.fl...  69.3 us
    reshape x1, local copies, waits for them, and re-layouts, block_terms(): bloch = bloch.reshape(n_modes, n_bands, n_bands, columns)  47.2 us
    psum x2, blocking collectives, on_device(): phonon = lax.psum(lax.psum(phon_local, 'row'), 'ka')  43.7 us
    dot_general x1, matrix products, block_terms(): jnp.einsum('bmjc,jnc->bmnc', modal, eig_k_cols, preferred_element_type=jn...  23 us
  transfers between devices with their start and end apart: 2, of which 0 were waited for; matrix products, arithmetic and copies ran while one was open for 4% of the time, Pallas kernels for 0%

profile of v2, /device:TPU:40, one launch (start us, length us, event | category | flops | bytes accessed | tf_op | source)
XLA Modules:
  0.0 457.2 jit_solution(1038445209698914054)
XLA Ops:
  7.2 1.7 copy.47
  9.0 1.8 copy.49
  11.2 0.7 convert_element_type.50
  11.8 1.3 dynamic-slice.8
  13.8 0.8 convert_dynamic-update-slice_fusion
  14.5 78.9 %all-reduce = f32[1024]{0:T(1024)S(1)} all-reduce(f32[1024]{0:T(1024)S(1)} %convert_dynamic-update-slice_fusion), channel_id=1, replica_groups=mesh['ka'=8,'pb'=16,'row'=4] {'ka','row'}, use_global_device_ids=true, to_apply=%add | all-reduce | flops 1024 | bytes 8192
  93.6 1.0 gather_fusion.2
  94.6 0.8 copy.79
  95.5 0.1 copy.62
  95.7 82.7 %all-gather = f32[32,32,24]{1,2,0:T(8,128)S(1)} all-gather(f32[1,32,24]{1,2,0:T(8,128)} %bitcast.93), channel_id=1, replica_groups=mesh['ka'=8,'pb'=16,'row'=4] {'ka','row'}, dimensions={0}, use_global_device_ids=true | all-gather | bytes 101376 | tf_op jit(solution)/shard_map/all_gather | solution.py:75
  178.4 0.2 copy.57
  178.8 0.1 copy.61
  178.9 0.1 copy.64
  179.0 0.7 gather_fusion.1
  179.8 0.1 copy.65
  180.0 0.8 constant_dynamic-slice_fusion.1
  180.8 2.2 broadcast_subtract_fusion
  182.9 0.9 dynamic-slice_bitcast_fusion
  183.9 0.1 copy.48
  184.0 3.5 gather_fusion
  187.6 8.0 %fusion.4 = bf16[20736,4,32]{0,2,1:T(8,128)(2,1)} fusion(bf16[4,64,20736]{2,0,1:T(4,128)(2,1)} %all-gather.6.cloned.1.call-done, f32[32]{0:T(128)S(1)} %get-tuple-element.18, f32[64]{0:T(128)S(1)} %get-tuple-element.15, f32[32]{0:T(128)S(1)} %get-tuple-element.19, f32[64]{0:T(128)S(1)} %get-tuple-element.16, f32[32]{0:T(128)S(1)} %get-tuple-element.17, ...), kind=kOutput, calls=%fused_computation.10 | convolution fusion | flops 342407168 | bytes 15926400 | tf_op jit(solution)/shard_map/qrf,rk->fqk/dot_general | solution.py:30
  195.6 47.2 %reshape.253 = bf16[36,24,24,128]{2,1,0,3:T(8,128)(2,1)} reshape(bf16[20736,4,32]{0,2,1:T(8,128)(2,1)} %fusion.4) | data formatting | bytes 10616832 | tf_op jit(solution)/shard_map/reshape | solution.py:33
  242.8 0.1 tile.10
  242.9 0.2 broadcast_in_dim.40.clone
  243.1 23.0 %convert_bitcast_fusion = bf16[36,24,24,128]{0,2,1,3:T(8,128)(2,1)} fusion(bf16[24,24,128,1]{0,1,3,2:T(8,128)(2,1)S(1)} %bitcast.86, bf16[36,36,128,1]{1,0,3,2:T(8,128)(2,1)S(1)} %bitcast.85, bf16[36,24,24,128]{2,1,0,3:T(8,128)(2,1)} %reshape.253), kind=kOutput, calls=%fused_computation.15 | convolution fusion | flops 323813376 | bytes 11096064 | tf_op jit(solution)/shard_map/bmjc,jnc->bmnc/dot_general | solution.py:39
  266.1 69.3 %multiply_reduce_fusion = (f32[36,128]{0,1:T(8,128)S(1)}, f32[24,128]{0,1:T(8,128)S(1)}) fusion(f32[24,24,128]{0,1,2:T(8,128)} %get-tuple-element.22, f32[24,128]{0,1:T(8,128)S(1)} %copy.63, f32[24,128]{0,1:T(8,128)S(1)} %copy.62, f32[36,128]{0,1:T(8,128)S(1)} %bitcast.90, f32[24,24,128]{0,1,2:T(8,128)} %get-tuple-element.23, ...), kind=kOutput, calls=%fused_computation.6 | convolution fusion | flops 159318528 | bytes 6119552 | tf_op jit(solution)/shard_map/imc,binc->bmnc/dot_general | solution.py:42
  335.5 69.8 %psum.21 = f32[32,24]{1,0:T(8,128)S(1)} all-reduce(f32[32,24]{1,0:T(8,128)S(1)} %multiply_bitcast_fusion.1), channel_id=1, replica_groups=mesh['ka'=8,'pb'=16,'row'=4] {'pb'}, use_global_device_ids=true, to_apply=%region_2.3 | all-reduce | flops 768 | bytes 6144 | tf_op jit(solution)/shard_map/psum | solution.py:104
  405.3 0.7 copy.67
  405.9 0.1 copy.78
  406.0 16.5 %psum.22 = f32[4,36]{0,1:T(8,128)S(1)} all-reduce(f32[4,36]{0,1:T(8,128)S(1)} %multiply_bitcast_fusion), channel_id=1, replica_groups=mesh['ka'=8,'pb'=16,'row'=4] {'row'}, use_global_device_ids=true, to_apply=%region_5.6 | all-reduce | flops 144 | bytes 1152 | tf_op jit(solution)/shard_map/psum | solution.py:103
  422.5 27.2 %psum.23 = f32[4,36]{0,1:T(8,128)S(1)} all-reduce(f32[4,36]{0,1:T(8,128)S(1)} %psum.22), channel_id=1, replica_groups=mesh['ka'=8,'pb'=16,'row'=4] {'ka'}, use_global_device_ids=true, to_apply=%region_6.7 | all-reduce | flops 144 | bytes 1152 | tf_op jit(solution)/shard_map/psum | solution.py:103
  449.7 0.7 copy.68
  (40 shorter events, 1.2 us)
Async XLA Ops:
  7.2 3.7 copy-start
  7.2 175.7 %all-gather.4.cloned.1.call-start = ((), (), s32[]{:S(2)}) async-start(), calls=%async_computation | async-start | bytes 6488064 | tf_op jit(solution)/shard_map/all_gather | solution.py:73
  9.0 178.6 %all-gather.6.cloned.1.call-start = ((), (), s32[]{:S(2)}) async-start(), calls=%async_computation.1 | async-start | bytes 10948608 | tf_op jit(solution)/shard_map/all_gather | solution.py:82
  243.1 23.0 %copy-start.2 = (f32[4,36]{1,0:T(4,128)S(1)}, f32[4,36]{1,0:T(4,128)}, u32[]{:S(2)}) copy-start(f32[4,36]{1,0:T(4,128)} %param.11) | copy-start | bytes 1732
  266.1 184.3 %copy-start.1 = (s32[4,1024]{1,0:T(4,128)S(1)}, s32[4,1024]{1,0:T(4,128)}, u32[]{:S(2)}) copy-start(s32[4,1024]{1,0:T(4,128)} %param.15) | copy-start | bytes 49156
Sparse Core Ops, SparseCore 0:
  11.1 75.5 all-gather.3
  89.9 93.6 all-gather.5
